TPU v7x, 32 devices: a whole 2x2x4 slice. The times are simulated.
32 devices in a mesh: band: 16 (over z, y, core), pw: 2 (over x).
Axes of the slice: x: 2, y: 2, z: 4, core: 2. Of those that a mesh axis runs over, the one named last changes fastest.
Arguments:
- mel: bfloat16 [32, 256, 32768], P('band', None, 'pw'), may hold values from -6 to 6
- pole_amp: bfloat16 [32768, 256], P('pw', 'band'), may hold values from 0.19921875 to 5
- pole_freq: bfloat16 [32768, 256], P('pw', 'band'), may hold values from 0.5 to 4
- band_energy: float32 [32], P('band'), may hold values from -3 to 3
- occupation: int32 [32], P('band'), may hold values from 0 to 1
- column_map: int32 [256], replicated, may hold values from 0 to 32767
- energies: float32 [2], replicated, may hold values from -2 to 2
Outputs:
- sigma: float32 [2, 256, 256], P(None, 'pw')
All inputs are finite; a program needn't handle non-finite values.
Results may differ from a plain program's by a relative error of at most 0.0055.
Values may be sent and summed in bfloat16 or wider, within the bound.
No kernel may reach another device: no remote copies, remote signals or barrier semaphores. Data moves between devices by JAX's collectives and lax.ppermute only.
A program may use at most 64 MiB of HBM per device.

v0:
```python
import math
import jax
import jax.numpy as jnp
from jax import lax
from jax.sharding import PartitionSpec as P

broadening = 0.4


def local(mel, pole_amp, pole_freq, band_energy, occupation, column_map, energies):
    row_count = mel.shape[2]
    offset = lax.axis_index("pw") * row_count
    local_index = column_map - offset
    inside = (local_index >= 0) & (local_index < row_count)
    picked = jnp.take(mel, jnp.clip(local_index, 0, row_count - 1), axis=2)
    picked = jnp.where(inside[None, None, :], picked, jnp.zeros_like(picked))
    chosen = lax.psum(picked, "pw").astype(jnp.float32).astype(jnp.bfloat16)
    branch_sign = (2 * occupation - 1).astype(jnp.float32)
    energy_count = energies.shape[0]
    band_count = mel.shape[0]
    pairing = (((1,), (1,)), ((), ()))
    whole_amp, whole_freq = (
        lax.all_gather(pole_amp, "band", axis=1, tiled=True),
        lax.all_gather(pole_freq, "band", axis=1, tiled=True),
    )
    amplitude = whole_amp.astype(jnp.float32)
    frequency = whole_freq.astype(jnp.float32)
    strength = amplitude / frequency
    column_blocks = [chosen[band_index] for band_index in range(band_count)]
    columns = jnp.concatenate(column_blocks, axis=1)
    updated = []
    for energy_index in range(energy_count):
        blocks = []
        for band_index in range(band_count):
            offset_gap = (
                energies[energy_index]
                - band_energy[band_index]
                + branch_sign[band_index] * frequency
            )
            screened = (
                strength * offset_gap / (offset_gap * offset_gap + broadening * broadening)
            ).astype(jnp.bfloat16)
            blocks.append(jnp.dot(mel[band_index], screened, preferred_element_type=jnp.float32))
        joined = jnp.concatenate(blocks, axis=1)
        upper = joined.astype(jnp.bfloat16)
        lower = (joined - upper.astype(jnp.float32)).astype(jnp.bfloat16)
        product = lax.dot_general(upper, columns, pairing, preferred_element_type=jnp.float32)
        product = product + lax.dot_general(
            lower, columns, pairing, preferred_element_type=jnp.float32
        )
        updated.append(product)
    partial_sigma = jnp.stack(updated)
    total_rows = row_count * lax.axis_size("pw")
    total_bands = band_count * lax.axis_size("band")
    partial_sigma = partial_sigma / math.sqrt(total_rows * column_map.shape[0] * total_bands)
    banded = lax.psum(partial_sigma, "band")
    return lax.psum_scatter(banded, "pw", scatter_dimension=1, tiled=True)


def solution(mesh):
    return jax.shard_map(
        local,
        mesh=mesh,
        in_specs=(
            P("band", None, "pw"),
            P("pw", "band"),
            P("pw", "band"),
            P("band"),
            P("band"),
            P(),
            P(),
        ),
        out_specs=P(None, "pw", None),
        check_vma=False,
    )
```

profile of v0, /device:TPU:1, one launch (start us, length us, event | category | flops | bytes accessed | tf_op | source)
XLA Modules:
  0.0 374.0 jit_solution(2522564181378667351)
XLA Ops:
  7.4 0.7 compare_and_fusion
  8.1 40.8 %copy.13 = bf16[2,256,16384]{1,0,2:T(2,128)(2,1)} copy(bf16[2,256,16384]{2,1,0:T(8,128)(2,1)} %param.7) | data formatting | bytes 33554432 | tf_op args[0]
  48.9 7.0 %gather_fusion = bf16[256,2,256]{2,1,0:T(2,128)(2,1)S(1)} fusion(bf16[2,256,16384]{1,0,2:T(2,128)(2,1)} %copy.13, s32[1024]{0:T(1024)S(1)} %pad_clamp_fusion), kind=kCustom, calls=%fused_computation | custom fusion | bytes 525312 | tf_op jit(solution)/shard_map/jit(_take)/gather | solution.py:15
  55.9 2.1 fusion.68
  58.0 0.0 all-reduce.3.cloned.1.call-update
  58.1 0.0 all-gather.3.cloned.1.call-start
  58.1 0.5 all-gather.3.cloned.1.call-update
  58.6 0.0 all-gather.5.cloned.1.call-start
  58.7 0.5 all-gather.5.cloned.1.call-update
  59.2 0.0 reduce-scatter.2.cloned.1.call-start
  59.3 0.6 fusion.78
  64.7 0.6 fusion.79
  65.3 18.0 %all-reduce.3.cloned.1.call-done = bf16[2,256,256]{1,0,2:T(2,128)(2,1)} async-done(((bf16[2,256,256]{1,0,2:T(2,128)(2,1)}), bf16[2,256,256]{1,0,2:T(2,128)(2,1)}) %all-reduce.3.cloned.1.call-update) | async-done | bytes 262160 | tf_op jit(solution)/shard_map/psum | solution.py:17
  83.3 1.5 fusion.77
  84.8 0.1 copy.14
  85.0 0.1 copy.15
  85.1 52.1 %all-gather.3.cloned.1.call-done = bf16[16384,256]{0,1:T(8,128)(2,1)} async-done(((bf16[16384,16]{0,1:T(8,128)(2,1)}), bf16[16384,256]{0,1:T(8,128)(2,1)}) %all-gather.3.cloned.1.call-update) | async-done | bytes 8388624 | tf_op jit(solution)/shard_map/all_gather | solution.py:23
  137.3 74.8 %all-gather.5.cloned.1.call-done = bf16[16384,256]{0,1:T(8,128)(2,1)} async-done(((bf16[16384,16]{0,1:T(8,128)(2,1)}), bf16[16384,256]{0,1:T(8,128)(2,1)}) %all-gather.5.cloned.1.call-update) | async-done | bytes 8388624 | tf_op jit(solution)/shard_map/all_gather | solution.py:24
  212.0 12.7 %fusion.47 = f32[256,256]{0,1:T(8,128)S(1)} fusion(bf16[2,256,16384]{2,1,0:T(8,128)(2,1)} %param.7, bf16[16384,256]{0,1:T(8,128)(2,1)} %all-gather.5.cloned.1.call-done, f32[]{:T(128)} %bitcast.12, f32[]{:T(128)} %bitcast.1, bf16[16384,256]{0,1:T(8,128)(2,1)} %all-gather.3.cloned.1.call-done), kind=kOutput, calls=%fused_computation.45 | convolution fusion | flops 2189426688 | bytes 25428992 | tf_op jit(solution)/shard_map/dot_general | solution.py:43
  224.8 12.8 %fusion.57 = f32[256,256]{0,1:T(8,128)S(1)} fusion(bf16[2,256,16384]{2,1,0:T(8,128)(2,1)} %param.7, bf16[16384,256]{0,1:T(8,128)(2,1)} %all-gather.5.cloned.1.call-done, f32[]{:T(128)} %bitcast.14, f32[]{:T(128)} %bitcast.5, bf16[16384,256]{0,1:T(8,128)(2,1)} %all-gather.3.cloned.1.call-done), kind=kOutput, calls=%fused_computation.47 | convolution fusion | flops 2189426688 | bytes 25428992 | tf_op jit(solution)/shard_map/dot_general | solution.py:43
  237.6 0.3 fusion.66
  237.9 0.3 fusion.40
  238.2 10.9 %fusion.42 = f32[256,256]{0,1:T(8,128)S(1)} fusion(bf16[2,256,16384]{2,1,0:T(8,128)(2,1)S(1)} %bitcast.41, bf16[16384,256]{0,1:T(8,128)(2,1)} %all-gather.5.cloned.1.call-done, f32[]{:T(128)} %bitcast.1, f32[]{:T(128)} %bitcast, bf16[16384,256]{0,1:T(8,128)(2,1)} %all-gather.3.cloned.1.call-done), kind=kOutput, calls=%fused_computation.44 | convolution fusion | flops 2189426688 | bytes 25427976 | tf_op jit(solution)/shard_map/dot_general | solution.py:43
  249.2 11.0 %fusion.52 = f32[256,256]{0,1:T(8,128)S(1)} fusion(bf16[2,256,16384]{2,1,0:T(8,128)(2,1)S(1)} %bitcast.41, bf16[16384,256]{0,1:T(8,128)(2,1)} %all-gather.5.cloned.1.call-done, f32[]{:T(128)} %bitcast.5, f32[]{:T(128)} %bitcast.4, bf16[16384,256]{0,1:T(8,128)(2,1)} %all-gather.3.cloned.1.call-done), kind=kOutput, calls=%fused_computation.46 | convolution fusion | flops 2189426688 | bytes 25427976 | tf_op jit(solution)/shard_map/dot_general | solution.py:43
  260.2 0.3 fusion.64
  260.5 0.3 fusion.41
  260.8 0.8 maximum_multiply_fusion
  261.6 0.0 all-reduce.5.cloned.1.call-start
  261.7 12.8 %reduce-scatter.2.cloned.1.call-done = f32[2,128,256]{2,1,0:T(8,128)} async-done(((f32[2,256,256]{2,1,0:T(8,128)}), f32[2,128,256]{2,1,0:T(8,128)}) %reduce-scatter.2.cloned.1.call-update) | async-done | bytes 262160 | tf_op jit(solution)/shard_map/reduce_scatter | solution.py:57
  274.5 0.0 all-reduce.5.cloned.1.call-update
  274.5 90.3 %all-reduce.5.cloned.1.call-done = f32[2,128,256]{2,1,0:T(8,128)} async-done(((f32[2,128,256]{2,1,0:T(8,128)}), f32[2,128,256]{2,1,0:T(8,128)}) %all-reduce.5.cloned.1.call-update) | async-done | bytes 262160 | tf_op jit(solution)/shard_map/psum | solution.py:56
  364.7 1.7 copy.18
  (19 shorter events, 0.1 us)
Async XLA Ops:
  7.4 76.0 %all-reduce.3.cloned.1.call-start = ((), (), s32[]{:S(2)}) async-start(), calls=%async_computation.3 | async-start | bytes 524288 | tf_op jit(solution)/shard_map/psum | solution.py:17
  8.1 51.2 %copy-start = (f32[2]{0:T(128)S(1)}, f32[2]{0:T(128)}, u32[]{:S(2)}) copy-start(f32[2]{0:T(128)} %param.13) | copy-start | bytes 28
  8.1 51.2 %copy-start.1 = (f32[2]{0:T(128)S(1)}, f32[2]{0:T(128)}, u32[]{:S(2)}) copy-start(f32[2]{0:T(128)} %param.10) | copy-start | bytes 28
  8.1 56.6 %copy-start.2 = (s32[2]{0:T(128)S(1)}, s32[2]{0:T(128)}, u32[]{:S(2)}) copy-start(s32[2]{0:T(128)} %param.11) | copy-start | bytes 28
  58.1 79.2 %all-gather.3.cloned.1.call-start = ((), (), s32[]{:S(2)}) async-start(), calls=%async_computation.1 | async-start | bytes 8912896 | tf_op jit(solution)/shard_map/all_gather | solution.py:23
  58.6 153.4 %all-gather.5.cloned.1.call-start = ((), (), s32[]{:S(2)}) async-start(), calls=%async_computation.2 | async-start | bytes 8912896 | tf_op jit(solution)/shard_map/all_gather | solution.py:24
  59.2 215.2 %reduce-scatter.2.cloned.1.call-start = ((), (), s32[]{:S(2)}) async-start(), calls=%async_computation.4 | async-start | bytes 786432 | tf_op jit(solution)/shard_map/reduce_scatter | solution.py:57
  212.0 26.2 %slice-start = ((s8[16777216]{0:T(1024)(128)(4,1)}), s8[4194304]{0:T(1024)(128)(4,1)S(1)}, s32[]{:S(2)}) async-start(s8[16777216]{0:T(1024)(128)(4,1)} %bitcast.40), calls=%async_computation.6 | async-start | bytes 8388608
  212.0 26.2 %slice-start.1 = ((s8[16777216]{0:T(1024)(128)(4,1)}), s8[4194304]{0:T(1024)(128)(4,1)S(1)}, s32[]{:S(2)}) async-start(s8[16777216]{0:T(1024)(128)(4,1)} %bitcast.40), calls=%async_computation.7 | async-start | bytes 8388608
  224.8 13.4 %slice-start.2 = ((s8[16777216]{0:T(1024)(128)(4,1)}), s8[4194304]{0:T(1024)(128)(4,1)S(1)}, s32[]{:S(2)}) async-start(s8[16777216]{0:T(1024)(128)(4,1)} %bitcast.40), calls=%async_computation.8 | async-start | bytes 8388608
  224.8 13.4 %slice-start.3 = ((s8[16777216]{0:T(1024)(128)(4,1)}), s8[4194304]{0:T(1024)(128)(4,1)S(1)}, s32[]{:S(2)}) async-start(s8[16777216]{0:T(1024)(128)(4,1)} %bitcast.40), calls=%async_computation.9 | async-start | bytes 8388608
  261.6 103.1 %all-reduce.5.cloned.1.call-start = ((), (), s32[]{:S(2)}) async-start(), calls=%async_computation.5 | async-start | bytes 524288 | tf_op jit(solution)/shard_map/psum | solution.py:56
Sparse Core Ops, SparseCore 0:
  58.2 25.1 all-reduce.2
  261.7 12.6 reduce-scatter.1
Sparse Core Ops, SparseCore 1:
  60.7 76.5 all-gather.2
  139.3 72.7 all-gather.4
  274.6 90.1 all-reduce.4
where the time goes:
time: 375 us; the launch traced here: 374 us
  waiting for transfers between devices  249 us (66%)
  local copies, waits for them, and re-layouts  52.5 us (14%)
  matrix products  48.6 us (13%)
  between operations  20 us (5%)
    psum x1, waiting for transfers between devices, local(): banded = lax.psum(partial_sigma, 'band')  90.3 us
    all_gather x1, waiting for transfers between devices, local(): lax.all_gather(pole_freq, 'band', axis=1, tiled=True)  74.8 us
    all_gather x1, waiting for transfers between devices, local(): lax.all_gather(pole_amp, 'band', axis=1, tiled=True)  52.1 us
    dot_general x4, matrix products, local(): jnp.dot(mel[band_index], screened, preferred_element_type=jnp.float32)  47.5 us
    unnamed x16, local copies, waits for them, and re-layouts  42.5 us
    psum x1, waiting for transfers between devices, local(): chosen = lax.psum(picked, 'pw').astype(jnp.float32).astype(jnp.bfloat16)  18 us
    reduce_scatter x1, waiting for transfers between devices, local(): return lax.psum_scatter(banded, 'pw', scatter_dimension=1, tiled=True)  12.8 us
  transfers between devices with their start and end apart: 5, of which 5 were waited for; matrix products, arithmetic and copies ran while one was open for 1% of the time, Pallas kernels for 0%

commit v1 on v0

--- a/solution.py
+++ b/solution.py
@@ -20,7 +20,9 @@
     band_count = mel.shape[0]
     pairing = (((1,), (1,)), ((), ()))
     whole_amp, whole_freq = (
-        lax.all_gather(pole_amp, "band", axis=1, tiled=True),
+        jnp.concatenate(
+            lax.all_to_all(jnp.stack([pole_amp] * lax.axis_size("band")), "band", 0, 0), axis=1
+        ),
         lax.all_gather(pole_freq, "band", axis=1, tiled=True),
     )
     amplitude = whole_amp.astype(jnp.float32)

time: 375 us -> 480 us (1.28)
  waiting for transfers between devices: 249 us -> 330 us
  other arithmetic: 3.68 us -> 16.5 us
  starting transfers between devices: 0.17 us -> 7.46 us
  local copies, waits for them, and re-layouts: 52.5 us -> 57.9 us
    all_gather x1, waiting for transfers between devices: 74.8 us -> 167 us  [local(): lax.all_gather(pole_freq, 'band', axis=1, tiled=True)]
    all_gather x1 -> x0, waiting for transfers between devices: 52.1 us -> none  [local(): lax.all_gather(pole_amp, 'band', axis=1, tiled=True)]
    reduce_scatter x1, waiting for transfers between devices: 12.8 us -> 45.2 us  [local(): return lax.psum_scatter(banded, 'pw', scatter_dimension=1, tiled=True)]
    all_to_all x0 -> x1, waiting for transfers between devices: none -> 20 us  [local(): lax.all_to_all(jnp.stack([pole_amp] * lax.axis_size('band')), 'band', 0, 0)]
    div x0 -> x1, other arithmetic: none -> 12.9 us  [local(): strength = amplitude / frequency]
    psum x1, waiting for transfers between devices: 18 us -> 7.07 us  [local(): chosen = lax.psum(picked, 'pw').astype(jnp.float32).astype(jnp.bfloat16)]
    all_to_all x0 -> x1, starting transfers between devices: none -> 7.34 us  [local(): lax.all_to_all(jnp.stack([pole_amp] * lax.axis_size('band')), 'band', 0, 0)]
    unnamed x16 -> x12, local copies, waits for them, and re-layouts: 42.5 us -> 43.7 us
  transfers between devices with their start and end apart: 5 -> 5, of which waited for: 5 -> 5; matrix products, arithmetic and copies ran while one was open for 1% -> 2% of each run, Pallas kernels for 0% -> 0%
where the time goes in v1:
time: 480 us; the launch traced here: 479 us
  waiting for transfers between devices  330 us (69%)
  local copies, waits for them, and re-layouts  57.9 us (12%)
  matrix products  47.1 us (10%)
  between operations  19.8 us (4%)
  other arithmetic  16.5 us (3%)
  starting transfers between devices  7.46 us (2%)
    all_gather x1, waiting for transfers between devices, local(): lax.all_gather(pole_freq, 'band', axis=1, tiled=True)  167 us
    psum x1, waiting for transfers between devices, local(): banded = lax.psum(partial_sigma, 'band')  90.2 us
    dot_general x4, matrix products, local(): jnp.dot(mel[band_index], screened, preferred_element_type=jnp.float32)  46 us
    reduce_scatter x1, waiting for transfers between devices, local(): return lax.psum_scatter(banded, 'pw', scatter_dimension=1, tiled=True)  45.2 us
    unnamed x12, local copies, waits for them, and re-layouts  43.7 us
    all_to_all x1, waiting for transfers between devices, local(): lax.all_to_all(jnp.stack([pole_amp] * lax.axis_size('band')), 'band', 0, 0)  20 us
    div x1, other arithmetic, local(): strength = amplitude / frequency  12.9 us
  transfers between devices with their start and end apart: 5, of which 5 were waited for; matrix products, arithmetic and copies ran while one was open for 2% of the time, Pallas kernels for 0%

profile of v1, /device:TPU:1, one launch (start us, length us, event | category | flops | bytes accessed | tf_op | source)
XLA Modules:
  0.0 478.7 jit_solution(10103770702678801218)
XLA Ops:
  7.4 0.7 compare_and_fusion
  8.1 40.8 %copy.13 = bf16[2,256,16384]{1,0,2:T(2,128)(2,1)} copy(bf16[2,256,16384]{2,1,0:T(8,128)(2,1)} %param.7) | data formatting | bytes 33554432 | tf_op args[0]
  48.9 7.0 %gather_fusion = bf16[256,2,256]{2,1,0:T(2,128)(2,1)S(1)} fusion(bf16[2,256,16384]{1,0,2:T(2,128)(2,1)} %copy.13, s32[1024]{0:T(1024)S(1)} %pad_clamp_fusion), kind=kCustom, calls=%fused_computation | custom fusion | bytes 525312 | tf_op jit(solution)/shard_map/jit(_take)/gather | solution.py:15
  55.9 2.1 fusion.68
  58.1 0.0 all-gather.2.cloned.1.call-start
  58.1 0.5 all-gather.2.cloned.1.call-update
  58.7 4.2 stack.8
  62.8 7.3 %all-to-all-start = ((bf16[16,16384,16]{1,2,0:T(8,128)(2,1)}), bf16[16,16384,16]{1,2,0:T(8,128)(2,1)}, u32[]{:S(2)}, u32[]{:S(2)}) async-start(bf16[16,16384,16]{1,2,0:T(8,128)(2,1)} %stack.8), calls=%async_computation | async-start | bytes 16777216 | tf_op jit(solution)/shard_map/all_to_all | solution.py:24
  70.2 0.0 reduce-scatter.2.cloned.1.call-start
  70.2 0.6 fusion.78
  75.7 0.6 fusion.79
  76.3 7.1 %all-reduce.3.cloned.1.call-done = bf16[2,256,256]{1,0,2:T(2,128)(2,1)} async-done(((bf16[2,256,256]{1,0,2:T(2,128)(2,1)}), bf16[2,256,256]{1,0,2:T(2,128)(2,1)}) %all-reduce.3.cloned.1.call-update) | async-done | bytes 262160 | tf_op jit(solution)/shard_map/psum | solution.py:17
  83.4 1.5 fusion.77
  84.9 0.1 copy.14
  85.0 0.1 copy.15
  85.2 166.8 %all-gather.2.cloned.1.call-done = bf16[16384,256]{0,1:T(8,128)(2,1)} async-done(((bf16[16384,16]{0,1:T(8,128)(2,1)}), bf16[16384,256]{0,1:T(8,128)(2,1)}) %all-gather.2.cloned.1.call-update) | async-done | bytes 8388624 | tf_op jit(solution)/shard_map/all_gather | solution.py:26
  252.0 20.0 %all-to-all-done = bf16[16,16384,16]{1,2,0:T(8,128)(2,1)} async-done(((bf16[16,16384,16]{1,2,0:T(8,128)(2,1)}), bf16[16,16384,16]{1,2,0:T(8,128)(2,1)}, u32[]{:S(2)}, u32[]{:S(2)}) %all-to-all-start) | async-done | bytes 8388640 | tf_op jit(solution)/shard_map/all_to_all | solution.py:24
  271.9 12.9 %convert_divide_fusion = f32[16384,256]{0,1:T(8,128)} fusion(bf16[16384,256]{0,1:T(8,128)(2,1)} %all-gather.2.cloned.1.call-done, bf16[16,16384,16]{1,2,0:T(8,128)(2,1)} %all-to-all-done), kind=kLoop, calls=%fused_computation.3 | loop fusion | flops 12582912 | bytes 33554432 | tf_op jit(solution)/shard_map/div | solution.py:30
  284.8 1.2 copy-done
  286.0 11.5 %fusion.57 = f32[256,256]{0,1:T(8,128)S(1)} fusion(bf16[2,256,16384]{2,1,0:T(8,128)(2,1)} %param.7, f32[16384,256]{0,1:T(8,128)} %convert_divide_fusion, bf16[16384,256]{0,1:T(8,128)(2,1)S(1)} %copy-done, f32[]{:T(128)} %bitcast.16, f32[]{:T(128)} %bitcast.7), kind=kOutput, calls=%fused_computation.47 | convolution fusion | flops 2181038080 | bytes 33817600 | tf_op jit(solution)/shard_map/dot_general | solution.py:45
  297.5 11.5 %fusion.47 = f32[256,256]{0,1:T(8,128)S(1)} fusion(bf16[2,256,16384]{2,1,0:T(8,128)(2,1)} %param.7, f32[16384,256]{0,1:T(8,128)} %convert_divide_fusion, bf16[16384,256]{0,1:T(8,128)(2,1)S(1)} %copy-done, f32[]{:T(128)} %bitcast.14, f32[]{:T(128)} %bitcast.3), kind=kOutput, calls=%fused_computation.45 | convolution fusion | flops 2181038080 | bytes 33817600 | tf_op jit(solution)/shard_map/dot_general | solution.py:45
  309.0 0.3 fusion.66
  309.3 0.3 fusion.40
  309.6 11.5 %fusion.52 = f32[256,256]{0,1:T(8,128)S(1)} fusion(bf16[2,256,16384]{2,1,0:T(8,128)(2,1)} %param.7, f32[16384,256]{0,1:T(8,128)} %convert_divide_fusion, bf16[16384,256]{0,1:T(8,128)(2,1)S(1)} %copy-done, f32[]{:T(128)} %bitcast.7, f32[]{:T(128)} %bitcast.6), kind=kOutput, calls=%fused_computation.46 | convolution fusion | flops 2181038080 | bytes 33817600 | tf_op jit(solution)/shard_map/dot_general | solution.py:45
  321.1 11.5 %fusion.42 = f32[256,256]{0,1:T(8,128)S(1)} fusion(bf16[2,256,16384]{2,1,0:T(8,128)(2,1)} %param.7, f32[16384,256]{0,1:T(8,128)} %convert_divide_fusion, bf16[16384,256]{0,1:T(8,128)(2,1)S(1)} %copy-done, f32[]{:T(128)} %bitcast.3, f32[]{:T(128)} %bitcast.2), kind=kOutput, calls=%fused_computation.44 | convolution fusion | flops 2181038080 | bytes 33817600 | tf_op jit(solution)/shard_map/dot_general | solution.py:45
  332.6 0.3 fusion.64
  332.9 0.3 fusion.41
  333.2 0.8 maximum_multiply_fusion
  334.0 0.0 all-reduce.5.cloned.1.call-start
  334.1 45.2 %reduce-scatter.2.cloned.1.call-done = f32[2,128,256]{2,1,0:T(8,128)} async-done(((f32[2,256,256]{2,1,0:T(8,128)}), f32[2,128,256]{2,1,0:T(8,128)}) %reduce-scatter.2.cloned.1.call-update) | async-done | bytes 262160 | tf_op jit(solution)/shard_map/reduce_scatter | solution.py:59
  379.3 90.2 %all-reduce.5.cloned.1.call-done = f32[2,128,256]{2,1,0:T(8,128)} async-done(((f32[2,128,256]{2,1,0:T(8,128)}), f32[2,128,256]{2,1,0:T(8,128)}) %all-reduce.5.cloned.1.call-update) | async-done | bytes 262160 | tf_op jit(solution)/shard_map/psum | solution.py:58
  469.6 1.7 copy.18
  (15 shorter events, 0.1 us)
Async XLA Ops:
  7.4 76.0 %all-reduce.3.cloned.1.call-start = ((), (), s32[]{:S(2)}) async-start(), calls=%async_computation.3 | async-start | bytes 524288 | tf_op jit(solution)/shard_map/psum | solution.py:17
  8.1 50.6 %copy-start.1 = (bf16[16384,16]{0,1:T(8,128)(2,1)S(1)}, bf16[16384,16]{0,1:T(8,128)(2,1)}, u32[]{:S(2)}) copy-start(bf16[16384,16]{0,1:T(8,128)(2,1)} %param.8) | copy-start | bytes 1572868
  48.9 21.4 %copy-start.2 = (f32[2]{0:T(128)S(1)}, f32[2]{0:T(128)}, u32[]{:S(2)}) copy-start(f32[2]{0:T(128)} %param.13) | copy-start | bytes 28
  48.9 21.4 %copy-start.3 = (f32[2]{0:T(128)S(1)}, f32[2]{0:T(128)}, u32[]{:S(2)}) copy-start(f32[2]{0:T(128)} %param.10) | copy-start | bytes 28
  48.9 26.8 %copy-start.4 = (s32[2]{0:T(128)S(1)}, s32[2]{0:T(128)}, u32[]{:S(2)}) copy-start(s32[2]{0:T(128)} %param.11) | copy-start | bytes 28
  58.1 193.9 %all-gather.2.cloned.1.call-start = ((), (), s32[]{:S(2)}) async-start(), calls=%async_computation.2 | async-start | bytes 8912896 | tf_op jit(solution)/shard_map/all_gather | solution.py:26
  62.8 209.1 %all-to-all-start = ((bf16[16,16384,16]{1,2,0:T(8,128)(2,1)}), bf16[16,16384,16]{1,2,0:T(8,128)(2,1)}, u32[]{:S(2)}, u32[]{:S(2)}) async-start(bf16[16,16384,16]{1,2,0:T(8,128)(2,1)} %stack.8), calls=%async_computation | async-start | bytes 16777216 | tf_op jit(solution)/shard_map/all_to_all | solution.py:24
  70.2 309.1 %reduce-scatter.2.cloned.1.call-start = ((), (), s32[]{:S(2)}) async-start(), calls=%async_computation.4 | async-start | bytes 786432 | tf_op jit(solution)/shard_map/reduce_scatter | solution.py:59
  271.9 14.1 %copy-start = (bf16[16384,256]{0,1:T(8,128)(2,1)S(1)}, bf16[16384,256]{0,1:T(8,128)(2,1)}, u32[]{:S(2)}) copy-start(bf16[16384,256]{0,1:T(8,128)(2,1)} %all-gather.2.cloned.1.call-done) | copy-start | bytes 25165828
  334.0 135.6 %all-reduce.5.cloned.1.call-start = ((), (), s32[]{:S(2)}) async-start(), calls=%async_computation.5 | async-start | bytes 524288 | tf_op jit(solution)/shard_map/psum | solution.py:58
Sparse Core Ops, SparseCore 0:
  58.2 25.1 all-reduce.2
  334.1 45.1 reduce-scatter.1
Sparse Core Ops, SparseCore 1:
  60.7 191.2 all-gather.1
  379.4 90.1 all-reduce.4
